TPU v7x, 32 devices: a whole 2x2x4 slice. The times are simulated.
32 devices in a mesh: dp: 16 (over z, y, core), seq: 2 (over x).
Axes of the slice: x: 2, y: 2, z: 4, core: 2. Of those that a mesh axis runs over, the one named last changes fastest.
Arguments:
- tokens: bfloat16 [16, 1024, 1024], P('dp', 'seq'), may hold values from -6 to 6
- cotangent: bfloat16 [16, 1024, 1024], P('dp', 'seq'), may hold values from -6 to 6
- doc_lengths: int32 [16, 8], P('dp'), may hold values from 1 to 512, 1024 in all within a row
- attn_gain: bfloat16 [1024], replicated, may hold values from 0.5 to 1.5
- w_query: bfloat16 [1024, 1024], replicated, may hold values from -0.1875 to 0.1875
- w_key: bfloat16 [1024, 512], replicated, may hold values from -0.1875 to 0.1875
- w_value: bfloat16 [1024, 512], replicated, may hold values from -0.1875 to 0.1875
- query_gain: bfloat16 [64], replicated, may hold values from 0.5 to 1.5
- key_gain: bfloat16 [64], replicated, may hold values from 0.5 to 1.5
- w_out: bfloat16 [1024, 1024], replicated, may hold values from -3 to 3
- ffn_gain: bfloat16 [1024], replicated, may hold values from 0.5 to 1.5
- w_gate: bfloat16 [1024, 4608], replicated, may hold values from -0.1875 to 0.1875
- w_up: bfloat16 [1024, 4608], replicated, may hold values from -0.1875 to 0.1875
- w_down: bfloat16 [4608, 1024], replicated, may hold values from -0.09375 to 0.09375
Outputs:
- output: float32 [16, 1024, 1024], P('dp', 'seq')
- d_tokens: float32 [16, 1024, 1024], P('dp', 'seq')
- d_attn_gain: float32 [1024], replicated
- d_w_query: float32 [1024, 1024], P('dp', 'seq')
- d_w_key: float32 [1024, 512], P('dp', 'seq')
- d_w_value: float32 [1024, 512], P('dp', 'seq')
- d_query_gain: float32 [64], replicated
- d_key_gain: float32 [64], replicated
- d_w_out: float32 [1024, 1024], P('dp', 'seq')
- d_ffn_gain: float32 [1024], replicated
- d_w_gate: float32 [1024, 4608], P('dp', 'seq')
- d_w_up: float32 [1024, 4608], P('dp', 'seq')
- d_w_down: float32 [4608, 1024], P('dp', 'seq')
Inputs may be any that keep to these rules, and one draw needn't show every extreme that they name: `doc_lengths`: each row's 8 documents fill its 1024 positions, and one of them is 512 long.
All inputs are finite; a program needn't handle non-finite values.
Results may differ from a plain program's by a relative error of at most 0.014.
Values may be sent and summed in bfloat16 or wider, within the bound.
No kernel may reach another device: no remote copies, remote signals or barrier semaphores. Data moves between devices by JAX's collectives and lax.ppermute only.
A program may use at most 256 MiB of HBM per device.

v0:
```python
import math
import jax
import jax.numpy as jnp
from jax import lax
from jax.sharding import PartitionSpec as P

EPSILON = 1e-06


def rms_scale(values, gain):
    return values * lax.rsqrt(jnp.mean(values * values, axis=-1, keepdims=True) + EPSILON) * gain


def norm_back(incoming, values, gain):
    inverse = lax.rsqrt(jnp.mean(values * values, axis=-1, keepdims=True) + EPSILON)
    unit = values * inverse
    scaled = incoming * gain
    d_values = inverse * (scaled - unit * jnp.mean(scaled * unit, axis=-1, keepdims=True))
    return (d_values, incoming * unit)


def rope_tables(first, count, width):
    half = width // 2
    spread = jnp.exp(jnp.arange(half, dtype=jnp.float32) * (-2.0 * math.log(1000000.0) / width))
    places = (first + jnp.arange(count, dtype=jnp.int32)).astype(jnp.float32)
    angles = places[:, None] * spread[None, :]
    return (jnp.cos(angles)[:, None, :], jnp.sin(angles)[:, None, :])


def rotate(values, cosine, sine):
    half = values.shape[-1] // 2
    first_half = values[..., :half]
    second_half = values[..., half:]
    return jnp.concatenate(
        [first_half * cosine - second_half * sine, second_half * cosine + first_half * sine],
        axis=-1,
    )


def reduce_grads(grads):
    partial_sum = lax.psum_scatter(grads, "dp", scatter_dimension=0, tiled=True)
    return lax.psum_scatter(partial_sum, "seq", scatter_dimension=1, tiled=True)


def body(
    tokens,
    cotangent,
    doc_lengths,
    attn_gain,
    w_query,
    w_key,
    w_value,
    query_gain,
    key_gain,
    w_out,
    ffn_gain,
    w_gate,
    w_up,
    w_down,
):
    shards = lax.axis_size("seq")
    local = tokens.shape[1]
    length = local * shards
    head_size = query_gain.shape[0]
    kv_count = w_key.shape[1] // head_size
    head_count = w_query.shape[1] // head_size
    group = head_count // kv_count
    kv_local = kv_count // shards
    block = min(512, length)
    num_blocks = length // block
    scale = head_size ** (-0.5)
    f32 = jnp.float32
    bf16 = jnp.bfloat16
    gain_attn = attn_gain.astype(f32)
    gain_query = query_gain.astype(f32)
    gain_key = key_gain.astype(f32)
    gain_ffn = ffn_gain.astype(f32)
    inputs = tokens[0].astype(f32)
    normed = rms_scale(inputs, gain_attn).astype(bf16)
    query_raw = jnp.dot(normed, w_query, preferred_element_type=f32).reshape(
        local, head_count, head_size
    )
    key_raw = jnp.dot(normed, w_key, preferred_element_type=f32).reshape(local, kv_count, head_size)
    values = (
        jnp.dot(normed, w_value, preferred_element_type=f32)
        .astype(bf16)
        .reshape(local, kv_count, head_size)
    )
    cosine, sine = rope_tables(lax.axis_index("seq") * local, local, head_size)
    query_rot = rotate(rms_scale(query_raw, gain_query), cosine, sine).astype(bf16)
    key_rot = rotate(rms_scale(key_raw, gain_key), cosine, sine).astype(bf16)
    packed_query = query_rot.reshape(local, kv_count, group * head_size)
    packed_kv = jnp.concatenate([key_rot, values], axis=2)
    query_heads, kv_heads = (
        lax.all_to_all(packed_query, "seq", split_axis=1, concat_axis=0, tiled=True),
        lax.all_to_all(packed_kv, "seq", split_axis=1, concat_axis=0, tiled=True),
    )
    query_all = query_heads.reshape(length, kv_local, group, head_size)
    key_all = kv_heads[:, :, :head_size]
    value_all = kv_heads[:, :, head_size:]
    positions = jnp.arange(length, dtype=jnp.int32)
    ends = jnp.cumsum(doc_lengths[0])
    segment = jnp.sum((ends[None, :] <= positions[:, None]).astype(jnp.int32), axis=1)
    starts = jnp.arange(num_blocks, dtype=jnp.int32) * block

    def allowed_at(begin):
        rows_here = begin + jnp.arange(block, dtype=jnp.int32)
        query_seg = lax.dynamic_slice_in_dim(segment, begin, block, 0)
        return (query_seg[:, None] == segment[None, :]) & (positions[None, :] <= rows_here[:, None])

    def block_scores(begin):
        query_block = lax.dynamic_slice_in_dim(query_all, begin, block, 0)
        scores = (
            jnp.einsum("qhgd,khd->hgqk", query_block, key_all, preferred_element_type=f32) * scale
        )
        return (query_block, jnp.where(allowed_at(begin), scores, -jnp.inf))

    def attend(begin):
        query_block, scores = block_scores(begin)
        top_score = jnp.max(scores, axis=-1, keepdims=True)
        expos = jnp.exp(scores - top_score)
        totals = jnp.sum(expos, axis=-1, keepdims=True)
        probs = (expos / totals).astype(bf16)
        result = jnp.einsum("hgqk,khd->qhgd", probs, value_all, preferred_element_type=f32)
        return (result.astype(bf16), top_score[..., 0] + jnp.log(totals[..., 0]))

    attended_heads, log_totals = lax.map(attend, starts)
    attended_heads = attended_heads.reshape(length, kv_local, group * head_size)
    attended = lax.all_to_all(
        attended_heads, "seq", split_axis=0, concat_axis=1, tiled=True
    ).reshape(local, head_count * head_size)
    hidden = inputs + jnp.dot(attended, w_out, preferred_element_type=f32)
    hnormed = rms_scale(hidden, gain_ffn).astype(bf16)
    gate = jnp.dot(hnormed, w_gate, preferred_element_type=f32)
    up_part = jnp.dot(hnormed, w_up, preferred_element_type=f32)
    act = (jax.nn.silu(gate) * up_part).astype(bf16)
    output = hidden + jnp.dot(act, w_down, preferred_element_type=f32)
    d_mlp = cotangent[0]
    grad_down = jnp.einsum("tf,td->fd", act, d_mlp, preferred_element_type=f32)
    d_act = jnp.einsum("td,fd->tf", d_mlp, w_down, preferred_element_type=f32)
    gate_again = jnp.dot(hnormed, w_gate, preferred_element_type=f32)
    up_again = jnp.dot(hnormed, w_up, preferred_element_type=f32)
    sigmoid_gate = jax.nn.sigmoid(gate_again)
    d_up = (d_act * gate_again * sigmoid_gate).astype(bf16)
    d_gate = (d_act * up_again * sigmoid_gate * (1.0 + gate_again * (1.0 - sigmoid_gate))).astype(
        bf16
    )
    grad_gate = jnp.einsum("td,tf->df", hnormed, d_gate, preferred_element_type=f32)
    grad_up = jnp.einsum("td,tf->df", hnormed, d_up, preferred_element_type=f32)
    ffn_sums = reduce_grads((grad_gate, grad_up, grad_down))
    d_hnormed = jnp.einsum("tf,df->td", d_gate, w_gate, preferred_element_type=f32) + jnp.einsum(
        "tf,df->td", d_up, w_up, preferred_element_type=f32
    )
    d_hidden_norm, ffn_gain_terms = norm_back(d_hnormed, hidden, gain_ffn)
    d_hidden = cotangent[0].astype(f32) + d_hidden_norm
    d_attn = d_hidden.astype(bf16)
    grad_out = jnp.einsum("tf,td->fd", attended, d_attn, preferred_element_type=f32)
    d_attended = jnp.einsum("td,fd->tf", d_attn, w_out, preferred_element_type=f32).astype(bf16)
    d_heads = lax.all_to_all(
        d_attended.reshape(local, kv_count, group * head_size),
        "seq",
        split_axis=1,
        concat_axis=0,
        tiled=True,
    )
    d_all = d_heads.reshape(length, kv_local, group, head_size)

    def attend_back(carry, item):
        begin, log_block = item
        query_block, scores = block_scores(begin)
        probs = jnp.exp(scores - log_block[..., None])
        d_block = lax.dynamic_slice_in_dim(d_all, begin, block, 0)
        d_probs = jnp.einsum("qhgd,khd->hgqk", d_block, value_all, preferred_element_type=f32)
        delta = jnp.sum(probs * d_probs, axis=-1, keepdims=True)
        d_scores = (scale * (probs * (d_probs - delta))).astype(bf16)
        d_query_block = jnp.einsum("hgqk,khd->qhgd", d_scores, key_all, preferred_element_type=f32)
        key_total = carry[0] + jnp.einsum(
            "hgqk,qhgd->khd", d_scores, query_block, preferred_element_type=f32
        )
        value_total = carry[1] + jnp.einsum(
            "hgqk,qhgd->khd", probs.astype(bf16), d_block, preferred_element_type=f32
        )
        return ((key_total, value_total), d_query_block.astype(bf16))

    empty = jnp.zeros((length, kv_local, head_size), f32)
    (d_keys, d_values), d_queries = lax.scan(attend_back, (empty, empty), (starts, log_totals))
    d_queries = d_queries.reshape(length, kv_local, group * head_size)
    d_kv = jnp.concatenate([d_keys.astype(bf16), d_values.astype(bf16)], axis=2)
    d_query_pos, d_kv_pos = (
        lax.all_to_all(d_queries, "seq", split_axis=0, concat_axis=1, tiled=True),
        lax.all_to_all(d_kv, "seq", split_axis=0, concat_axis=1, tiled=True),
    )
    d_query_rot = d_query_pos.reshape(local, head_count, head_size).astype(f32)
    d_query_raw, query_gain_terms = norm_back(
        rotate(d_query_rot, cosine, -sine), query_raw, gain_query
    )
    d_query_low = d_query_raw.reshape(local, head_count * head_size).astype(bf16)
    d_key_rot = d_kv_pos[:, :, :head_size].astype(f32)
    d_key_raw, key_gain_terms = norm_back(rotate(d_key_rot, cosine, -sine), key_raw, gain_key)
    d_key_low = d_key_raw.reshape(local, kv_count * head_size).astype(bf16)
    d_value_low = d_kv_pos[:, :, head_size:].reshape(local, kv_count * head_size)
    grad_query = jnp.einsum("td,tf->df", normed, d_query_low, preferred_element_type=f32)
    grad_key = jnp.einsum("td,tf->df", normed, d_key_low, preferred_element_type=f32)
    grad_value = jnp.einsum("td,tf->df", normed, d_value_low, preferred_element_type=f32)
    d_normed = jnp.einsum("tf,df->td", d_query_low, w_query, preferred_element_type=f32)
    d_normed = d_normed + jnp.einsum("tf,df->td", d_key_low, w_key, preferred_element_type=f32)
    d_normed = d_normed + jnp.einsum("tf,df->td", d_value_low, w_value, preferred_element_type=f32)
    d_input_norm, attn_gain_terms = norm_back(d_normed, inputs, gain_attn)
    d_inputs = d_hidden + d_input_norm
    attn_sums = reduce_grads((grad_query, grad_key, grad_value, grad_out))
    gain_totals = lax.psum(
        (
            jnp.sum(attn_gain_terms, axis=0),
            jnp.sum(query_gain_terms, axis=(0, 1)),
            jnp.sum(key_gain_terms, axis=(0, 1)),
            jnp.sum(ffn_gain_terms, axis=0),
        ),
        ("dp", "seq"),
    )
    return (
        output[None],
        d_inputs[None],
        gain_totals[0],
        attn_sums[0],
        attn_sums[1],
        attn_sums[2],
        gain_totals[1],
        gain_totals[2],
        attn_sums[3],
        gain_totals[3],
        ffn_sums[0],
        ffn_sums[1],
        ffn_sums[2],
    )


def solution(mesh):
    return jax.shard_map(
        body,
        mesh=mesh,
        in_specs=(
            P("dp", "seq", None),
            P("dp", "seq", None),
            P("dp", None),
            P(),
            P(),
            P(),
            P(),
            P(),
            P(),
            P(),
            P(),
            P(),
            P(),
            P(),
        ),
        out_specs=(
            P("dp", "seq", None),
            P("dp", "seq", None),
            P(),
            P("dp", "seq"),
            P("dp", "seq"),
            P("dp", "seq"),
            P(),
            P(),
            P("dp", "seq"),
            P(),
            P("dp", "seq"),
            P("dp", "seq"),
            P("dp", "seq"),
        ),
        check_vma=False,
    )
```

profile of v0, /device:TPU:0, one launch (start us, length us, event | category | flops | bytes accessed | tf_op | source)
XLA Modules:
  0.0 1398.1 jit_solution(11515140757117083535)
XLA Ops:
  11.9 3.0 multiply_reduce_fusion.8
  19.7 4.4 all-to-all-start.1
  24.1 3.9 copy.93
  28.0 3.0 multiply_reduce_fusion.5
  33.7 5.5 all-to-all-done.1
  39.2 4.6 all-to-all-start
  44.2 2.3 copy.124
  49.3 7.9 all-to-all-done
  57.3 3.3 copy.125
  60.5 2.6 reshape.334
  64.2 36.4 %while.28 = (s32[]{:T(128)}, bf16[2,512,4,2,64]{1,4,3,2,0:T(8,128)(2,1)}, f32[2,4,2,512]{3,2,1,0:T(2,128)S(1)}, s32[2]{0:T(128)S(1)}, s32[1024]{0:T(1024)S(1)}, ...) while((s32[]{:T(128)}, ...), condition=%wide.region_8.9_spmd.clone, body=%wide.region_5.8_spmd.clone.sunk | while | flops 1125904896 | bytes 54672044 | solution.py:127
  68.0 4.4 bitcast_reduce_fusion.2
  72.5 4.3 fusion.161
  76.8 5.6 fusion.162
  86.2 4.4 bitcast_reduce_fusion.2
  90.6 4.3 fusion.161
  95.0 5.6 fusion.162
  100.6 6.1 copy.115
  106.7 5.1 reshape.352
  111.8 4.9 all-to-all-start.2
  116.7 12.4 all-to-all-done.2
  129.1 2.3 copy.99
  131.5 2.3 copy.100
  133.8 2.7 multiply_reduce_fusion.4
  138.4 7.6 fusion.102
  146.0 7.4 fusion.103
  153.4 20.4 %multiply_convert_fusion = (bf16[512,4608]{1,0:T(8,128)(2,1)}, bf16[512,4608]{1,0:T(8,128)(2,1)}, bf16[512,4608]{1,0:T(8,128)(2,1)}) fusion(f32[512,4608]{1,0:T(8,128)} %fusion.102, f32[512,4608]{1,0:T(8,128)} %fusion.103, bf16[4608,1024]{1,0:T(8,128)(2,1)} %param.31, bf16[1,512,1024]{2,1,0:T(8,128)(2,1)S(1)} %copy-done.27), kind=kOutput, calls=%fused_computation.63 | convolution fusion | flops 4869586944 | bytes 43515904 | tf_op jit(solution)/shard_map/td,fd->tf/dot_general | solution.py:140
  173.8 9.2 fusion.104
  183.0 8.8 multiply_reduce_fusion
  194.9 3.6 all-to-all-start.3
  198.6 11.4 all-to-all-done.3
  215.0 155.5 %while.29 = (s32[]{:T(128)}, f32[1024,4,64]{0,2,1:T(8,128)}, f32[1024,4,64]{0,2,1:T(8,128)S(1)}, bf16[2,512,4,2,64]{1,4,3,2,0:T(8,128)(2,1)}, s32[2]{0:T(128)S(1...) while((s32[]{:T(128)}, f32[1024,4,64]{0,2,1:T(8,128)}, ...), condition=%wide.region_13.14_spmd.clone, body=%wide.region_11.13_spmd.clone.sunk | while | flops 2745969152 | bytes 194050784 | solution.py:186
  218.8 9.6 fusion.172
  228.4 8.2 fusion.173
  236.6 25.5 %fusion.176 = bf16[2,512,4,2,64]{1,4,3,2,0:T(8,128)(2,1)} fusion(bf16[2,512,4,2,64]{1,4,3,2,0:T(8,128)(2,1)} %get-tuple-element.434, s32[]{:T(128)} %get-tuple-element.431, f32[4,2,512,1024]{3,2,1,0:T(8,128)} %fusion.172, f32[4,512,2,1024]{3,1,2,0:T(8,128)} %fusion.173, bf16[1024,4,64]{0,2,1:T(8,128)(2,1)S(1)} %get-tuple-element.452), kind=kOutput, calls=%fused_computation.44.clone.1 | convolution fusion | flops 558109696 | bytes 68157952 | tf_op jit(solution)/shard_map/while/body/eval_jaxpr/hgqk,khd->qhgd/dot_general | solution.py:176
  262.1 22.9 %fusion.174 = f32[1024,4,64]{0,2,1:T(8,128)} fusion(f32[4,2,512,1024]{3,2,1,0:T(8,128)} %fusion.172, f32[4,512,2,1024]{3,1,2,0:T(8,128)} %fusion.173, f32[1024,4,64]{0,2,1:T(8,128)} %get-tuple-element.432, pred[]{:T(512)S(6)} %compare.3, bf16[1024,4,2,64]{0,3,2,1:T(8,128)(2,1)} %get-tuple-element.450, s32[]{:T(128)S(6)} %select_n.56), kind=kOutput, calls=%fused_computation.39.clone.1 | convolution fusion | flops 558371840 | bytes 69730312 | tf_op jit(solution)/shard_map/while/body/eval_jaxpr/hgqk,qhgd->khd/dot_general | solution.py:177
  284.9 7.6 fusion.175
  296.4 9.6 fusion.172
  306.0 8.2 fusion.173
  314.2 25.5 %fusion.176 = bf16[2,512,4,2,64]{1,4,3,2,0:T(8,128)(2,1)} fusion(bf16[2,512,4,2,64]{1,4,3,2,0:T(8,128)(2,1)} %get-tuple-element.434, s32[]{:T(128)} %get-tuple-element.431, f32[4,2,512,1024]{3,2,1,0:T(8,128)} %fusion.172, f32[4,512,2,1024]{3,1,2,0:T(8,128)} %fusion.173, bf16[1024,4,64]{0,2,1:T(8,128)(2,1)S(1)} %get-tuple-element.452), kind=kOutput, calls=%fused_computation.44.clone.1 | convolution fusion | flops 558109696 | bytes 68157952 | tf_op jit(solution)/shard_map/while/body/eval_jaxpr/hgqk,khd->qhgd/dot_general | solution.py:176
  339.7 23.2 %fusion.174 = f32[1024,4,64]{0,2,1:T(8,128)} fusion(f32[4,2,512,1024]{3,2,1,0:T(8,128)} %fusion.172, f32[4,512,2,1024]{3,1,2,0:T(8,128)} %fusion.173, f32[1024,4,64]{0,2,1:T(8,128)} %get-tuple-element.432, pred[]{:T(512)S(6)} %compare.3, bf16[1024,4,2,64]{0,3,2,1:T(8,128)(2,1)} %get-tuple-element.450, s32[]{:T(128)S(6)} %select_n.56), kind=kOutput, calls=%fused_computation.39.clone.1 | convolution fusion | flops 558371840 | bytes 69730312 | tf_op jit(solution)/shard_map/while/body/eval_jaxpr/hgqk,qhgd->khd/dot_general | solution.py:177
  362.8 7.6 fusion.175
  372.6 13.2 all_to_all.90
  391.6 3.5 fusion.85
  395.1 4.5 fusion.91
  399.8 4.6 copy.116
  406.1 13.2 all_to_all.91
  426.2 3.5 fusion.83
  430.9 11.6 fusion.107
  442.6 11.8 fusion.108
  455.6 11.7 fusion.75
  468.1 49.3 %reduce-scatter.23.cloned.1.call-done = f32[64,512]{1,0:T(8,128)} async-done(((f32[1024,512]{1,0:T(8,128)}), f32[64,512]{1,0:T(8,128)}) %reduce-scatter.23.cloned.1.call-update) | async-done | bytes 131088 | tf_op jit(solution)/shard_map/reduce_scatter | solution.py:41
  517.4 75.6 %reduce-scatter.27.cloned.1.call-done = f32[64,1024]{1,0:T(8,128)} async-done(((f32[1024,1024]{1,0:T(8,128)}), f32[64,1024]{1,0:T(8,128)}) %reduce-scatter.27.cloned.1.call-update) | async-done | bytes 262160 | tf_op jit(solution)/shard_map/reduce_scatter | solution.py:41
  593.1 75.9 %reduce-scatter.15.cloned.1.call-done = f32[64,1024]{1,0:T(8,128)} async-done(((f32[1024,1024]{1,0:T(8,128)}), f32[64,1024]{1,0:T(8,128)}) %reduce-scatter.15.cloned.1.call-update) | async-done | bytes 262160 | tf_op jit(solution)/shard_map/reduce_scatter | solution.py:41
  669.1 197.7 %reduce-scatter.31.cloned.1.call-done = f32[64,4608]{1,0:T(8,128)} async-done(((f32[1024,4608]{1,0:T(8,128)}), f32[64,4608]{1,0:T(8,128)}) %reduce-scatter.31.cloned.1.call-update) | async-done | bytes 1179664 | tf_op jit(solution)/shard_map/reduce_scatter | solution.py:41
  866.8 197.8 %reduce-scatter.35.cloned.1.call-done = f32[64,4608]{1,0:T(8,128)} async-done(((f32[1024,4608]{1,0:T(8,128)}), f32[64,4608]{1,0:T(8,128)}) %reduce-scatter.35.cloned.1.call-update) | async-done | bytes 1179664 | tf_op jit(solution)/shard_map/reduce_scatter | solution.py:41
  1064.7 198.1 %reduce-scatter.39.cloned.1.call-done = f32[288,1024]{1,0:T(8,128)} async-done(((f32[4608,1024]{1,0:T(8,128)}), f32[288,1024]{1,0:T(8,128)}) %reduce-scatter.39.cloned.1.call-update) | async-done | bytes 1179664 | tf_op jit(solution)/shard_map/reduce_scatter | solution.py:41
  1262.9 10.1 add_bitcast_fusion
  1276.2 2.6 fusion.69
  1278.8 39.5 %all-reduce = (f32[1024]{0:T(1024)}, f32[64]{0:T(128)}, f32[64]{0:T(128)}, f32[1024]{0:T(1024)}) all-reduce(f32[1024]{0:T(1024)S(1)} %get-tuple-element.190, f32[64]{0:T(128)S(1)} %get-tuple-element.186, f32[64]{0:T(128)S(1)} %get-tuple-element.192, f32[1024]{0:T(1024)S(1)} %copy-done.46), channel_id=1, replica_groups=mesh['dp'=16,'seq'=2] {'dp','seq'}, use_global_device_ids=true, to_apply=%region_18.19 | all-reduce | flops 2176 | bytes 17408 | tf_op jit(solution)/shard_map/psum | solution.py:211
  1318.3 4.2 fusion.68
  1322.6 19.4 %reduce-scatter.33.cloned.1.call-done = f32[64,2304]{1,0:T(8,128)} async-done(((f32[64,4608]{1,0:T(8,128)}), f32[64,2304]{1,0:T(8,128)}) %reduce-scatter.33.cloned.1.call-update) | async-done | bytes 589840 | tf_op jit(solution)/shard_map/reduce_scatter | solution.py:42
  1342.0 24.7 %reduce-scatter.37.cloned.1.call-done = f32[64,2304]{1,0:T(8,128)} async-done(((f32[64,4608]{1,0:T(8,128)}), f32[64,2304]{1,0:T(8,128)}) %reduce-scatter.37.cloned.1.call-update) | async-done | bytes 589840 | tf_op jit(solution)/shard_map/reduce_scatter | solution.py:42
  1366.7 24.4 %reduce-scatter.41.cloned.1.call-done = f32[288,512]{1,0:T(8,128)} async-done(((f32[288,1024]{1,0:T(8,128)}), f32[288,512]{1,0:T(8,128)}) %reduce-scatter.41.cloned.1.call-update) | async-done | bytes 589840 | tf_op jit(solution)/shard_map/reduce_scatter | solution.py:42
  (223 shorter events, 57.2 us)
Async XLA Ops:
  7.2 126.6 %copy-start = (bf16[1024,1024]{1,0:T(8,128)(2,1)S(1)}, bf16[1024,1024]{1,0:T(8,128)(2,1)}, u32[]{:S(2)}) copy-start(bf16[1024,1024]{1,0:T(8,128)(2,1)} %param.27) | copy-start | bytes 6291460
  7.2 4.7 copy-start.2
  8.9 19.1 %copy-start.40 = (f32[512]{0:T(512)}, f32[512]{0:T(512)S(1)}, u32[]{:S(2)}) copy-start(f32[512]{0:T(512)S(1)} %add_rsqrt_fusion.3) | copy-start | bytes 6148
  9.6 18.4 %copy-start.38 = (f32[1024]{0:T(1024)}, f32[1024]{0:T(1024)S(1)}, u32[]{:S(2)}) copy-start(f32[1024]{0:T(1024)S(1)} %convert_element_type.137) | copy-start | bytes 12292
  11.9 3.1 copy-start.49
  14.9 3.4 copy-start.36
  15.0 3.4 copy-start.44
  15.0 3.1 copy-start.16
  18.1 13.4 copy-start.24
  19.7 19.6 %all-to-all-start.1 = ((bf16[512,8,128]{0,2,1:T(8,128)(2,1)}), bf16[512,8,128]{0,2,1:T(8,128)(2,1)}, u32[]{:S(2)}, u32[]{:S(2)}) async-start(bf16[512,8,128]{0,2,1:T(8,128)(2,1)} %pad_maximum_fusion.2), calls=%async_computation.1 | async-start | bytes 2097152 | tf_op jit(solution)/shard_map/all_to_all | solution.py:96
  28.0 3.0 copy-start.50
  31.0 1.3 copy-start.7
  32.7 11.2 copy-start.51
  39.2 18.0 %all-to-all-start = ((bf16[512,8,128]{0,2,1:T(8,128)(2,1)}), bf16[512,8,128]{0,2,1:T(8,128)(2,1)}, u32[]{:S(2)}, u32[]{:S(2)}) async-start(bf16[512,8,128]{0,2,1:T(8,128)(2,1)} %bitcast.7), calls=%async_computation | async-start | bytes 2097152 | tf_op jit(solution)/shard_map/all_to_all | solution.py:95
  100.6 11.2 copy-start.5
  100.6 11.2 copy-start.34
  106.7 10.0 copy-start.47
  111.8 17.3 %all-to-all-start.2 = ((bf16[1024,4,128]{2,1,0:T(4,128)(2,1)}), bf16[1024,4,128]{2,1,0:T(4,128)(2,1)}, u32[]{:S(2)}, u32[]{:S(2)}) async-start(bf16[1024,4,128]{2,1,0:T(4,128)(2,1)} %reshape.352), calls=%async_computation.2 | async-start | bytes 2097152 | tf_op jit(solution)/shard_map/all_to_all | solution.py:129
  116.7 17.1 %copy-start.3 = (bf16[1,512,1024]{2,1,0:T(8,128)(2,1)S(1)}, bf16[1,512,1024]{2,1,0:T(8,128)(2,1)}, u32[]{:S(2)}) copy-start(bf16[1,512,1024]{2,1,0:T(8,128)(2,1)} %param.18) | copy-start | bytes 3145732
  133.8 4.6 copy-start.48
  136.5 1.3 copy-start.11
  137.8 8.1 slice-start
  138.4 7.6 copy-start.14
  138.4 7.6 slice-start.1
  138.4 7.6 slice-start.2
  146.0 7.4 copy-start.27
  173.8 9.2 copy-start.12
  173.8 9.2 copy-start.21
  192.4 1.4 copy-start.9
  194.9 15.1 %all-to-all-start.3 = ((bf16[512,8,128]{2,0,1:T(8,128)(2,1)}), bf16[512,8,128]{2,0,1:T(8,128)(2,1)S(1)}, u32[]{:S(2)}, u32[]{:S(2)}) async-start(bf16[512,8,128]{2,0,1:T(8,128)(2,1)} %bitcast.254), calls=%async_computation.3 | async-start | bytes 2097152 | tf_op jit(solution)/shard_map/all_to_all | solution.py:159
  198.5 268.9 %reduce-scatter.19.cloned.1.call-start = ((), (), s32[]{:S(2)}) async-start(), calls=%async_computation.22 | async-start | bytes 2228224 | tf_op jit(solution)/shard_map/reduce_scatter | solution.py:41
  212.0 3.0 copy-start.6
  212.0 3.0 copy-start.35
  385.8 1.7 copy-start.25
  385.8 1.7 copy-start.31
  386.5 1.4 copy-start.17
  386.5 1.4 copy-start.37
  386.5 1.4 copy-start.45
  388.7 2.8 copy-start.19
  391.5 125.9 %reduce-scatter.23.cloned.1.call-start = ((), (), s32[]{:S(2)}) async-start(), calls=%async_computation.24 | async-start | bytes 2228224 | tf_op jit(solution)/shard_map/reduce_scatter | solution.py:41
  391.5 3.6 copy-start.10
  395.1 197.9 %reduce-scatter.27.cloned.1.call-start = ((), (), s32[]{:S(2)}) async-start(), calls=%async_computation.26 | async-start | bytes 4456448 | tf_op jit(solution)/shard_map/reduce_scatter | solution.py:41
  399.7 269.3 %reduce-scatter.15.cloned.1.call-start = ((), (), s32[]{:S(2)}) async-start(), calls=%async_computation.20 | async-start | bytes 4456448 | tf_op jit(solution)/shard_map/reduce_scatter | solution.py:41
  421.4 2.2 copy-start.8
  421.4 2.2 copy-start.33
  421.4 2.2 copy-start.43
  429.7 437.0 %reduce-scatter.31.cloned.1.call-start = ((), (), s32[]{:S(2)}) async-start(), calls=%async_computation.28 | async-start | bytes 20054016 | tf_op jit(solution)/shard_map/reduce_scatter | solution.py:41
  442.5 622.1 %reduce-scatter.35.cloned.1.call-start = ((), (), s32[]{:S(2)}) async-start(), calls=%async_computation.30 | async-start | bytes 20054016 | tf_op jit(solution)/shard_map/reduce_scatter | solution.py:41
  454.4 808.4 %reduce-scatter.39.cloned.1.call-start = ((), (), s32[]{:S(2)}) async-start(), calls=%async_computation.32 | async-start | bytes 20054016 | tf_op jit(solution)/shard_map/reduce_scatter | solution.py:41
  467.3 855.2 %reduce-scatter.21.cloned.1.call-start = ((), (), s32[]{:S(2)}) async-start(), calls=%async_computation.23 | async-start | bytes 196608 | tf_op jit(solution)/shard_map/reduce_scatter | solution.py:42
  468.1 854.5 %reduce-scatter.25.cloned.1.call-start = ((), (), s32[]{:S(2)}) async-start(), calls=%async_computation.25 | async-start | bytes 196608 | tf_op jit(solution)/shard_map/reduce_scatter | solution.py:42
  517.4 745.5 %copy-start.13 = (f32[512,1024]{1,0:T(8,128)S(1)}, f32[512,1024]{1,0:T(8,128)}, u32[]{:S(2)}) copy-start(f32[512,1024]{1,0:T(8,128)} %copy-done.11) | copy-start | bytes 6291460
  517.4 805.2 %reduce-scatter.29.cloned.1.call-start = ((), (), s32[]{:S(2)}) async-start(), calls=%async_computation.27 | async-start | bytes 393216 | tf_op jit(solution)/shard_map/reduce_scatter | solution.py:42
  593.0 729.5 %reduce-scatter.17.cloned.1.call-start = ((), (), s32[]{:S(2)}) async-start(), calls=%async_computation.21 | async-start | bytes 393216 | tf_op jit(solution)/shard_map/reduce_scatter | solution.py:42
  669.0 672.9 %reduce-scatter.33.cloned.1.call-start = ((), (), s32[]{:S(2)}) async-start(), calls=%async_computation.29 | async-start | bytes 1769472 | tf_op jit(solution)/shard_map/reduce_scatter | solution.py:42
  866.8 499.9 %reduce-scatter.37.cloned.1.call-start = ((), (), s32[]{:S(2)}) async-start(), calls=%async_computation.31 | async-start | bytes 1769472 | tf_op jit(solution)/shard_map/reduce_scatter | solution.py:42
  1064.6 326.5 %reduce-scatter.41.cloned.1.call-start = ((), (), s32[]{:S(2)}) async-start(), calls=%async_computation.33 | async-start | bytes 1769472 | tf_op jit(solution)/shard_map/reduce_scatter | solution.py:42
  1262.9 10.1 copy-start.20
  1262.9 10.1 copy-start.22
  1272.9 1.6 copy-start.23
  1273.0 1.9 copy-start.30
  1274.8 1.4 copy-start.26
  1276.2 2.6 copy-start.46
  1318.3 72.8 %copy-start.1 = (bf16[1024,1024]{1,0:T(8,128)(2,1)S(1)}, bf16[1024,1024]{1,0:T(8,128)(2,1)}, u32[]{:S(2)}) copy-start(bf16[1024,1024]{1,0:T(8,128)(2,1)} %param.27) | copy-start | bytes 6291460
  (9 other events, 11.1 us)
Sparse Core Ops, SparseCore 0:
  391.6 60.9 reduce-scatter.18
  456.8 60.5 reduce-scatter.22
  521.2 71.7 reduce-scatter.26
  597.2 71.7 reduce-scatter.14
  673.0 193.7 reduce-scatter.30
  870.7 193.8 reduce-scatter.34
  1068.7 194.0 reduce-scatter.38
  1265.6 9.3 reduce-scatter.20
  1277.8 10.5 reduce-scatter.24
  1291.1 11.3 reduce-scatter.28
  1305.3 11.8 reduce-scatter.16
  1319.8 22.0 reduce-scatter.32
  1344.9 21.7 reduce-scatter.36
  1369.4 21.7 reduce-scatter.40
where the time goes:
time: 1400 us
  waiting for transfers between devices  901 us (64%)
  matrix products  297 us (21%)
  blocking collectives  65.9 us (5%)
  local copies, waits for them, and re-layouts  60.8 us (4%)
  other arithmetic  32.4 us (2%)
  starting transfers between devices  18 us (1%)
  between operations  15.1 us (1%)
    reduce_scatter x7, waiting for transfers between devices, reduce_grads(): partial_sum = lax.psum_scatter(grads, 'dp', scatter_dimension=0, tiled=True)  794 us
    reduce_scatter x7, waiting for transfers between devices, reduce_grads(): return lax.psum_scatter(partial_sum, 'seq', scatter_dimension=1, tiled=True)  68.6 us
    dot_general x2, matrix products, attend_back(): jnp.einsum('hgqk,khd->qhgd', d_scores, key_all, preferred_element_type=f32)  50.9 us
    dot_general x2, matrix products, attend_back(): jnp.einsum('hgqk,qhgd->khd', d_scores, query_block, preferred_element_typ...  46 us
    psum x1, blocking collectives, body(): lax.psum((jnp.sum(attn_gain_terms, axis=0), jnp.sum(query_gain_terms, axi...  39.5 us
  transfers between devices with their start and end apart: 18, of which 13 were waited for; matrix products, arithmetic and copies ran while one was open for 6% of the time, Pallas kernels for 0%

commit v1 on v0

--- a/solution.py
+++ b/solution.py
@@ -209,13 +209,16 @@
     d_inputs = d_hidden + d_input_norm
     attn_sums = reduce_grads((grad_query, grad_key, grad_value, grad_out))
     gain_totals = lax.psum(
-        (
-            jnp.sum(attn_gain_terms, axis=0),
-            jnp.sum(query_gain_terms, axis=(0, 1)),
-            jnp.sum(key_gain_terms, axis=(0, 1)),
-            jnp.sum(ffn_gain_terms, axis=0),
+        lax.psum(
+            (
+                jnp.sum(attn_gain_terms, axis=0),
+                jnp.sum(query_gain_terms, axis=(0, 1)),
+                jnp.sum(key_gain_terms, axis=(0, 1)),
+                jnp.sum(ffn_gain_terms, axis=0),
+            ),
+            "dp",
         ),
-        ("dp", "seq"),
+        "seq",
     )
     return (
         output[None],

time: 1400 us -> 1400 us (level)
  no operation moved by 1% of the time
where the time goes in v1:
time: 1400 us
  waiting for transfers between devices  902 us (64%)
  matrix products  297 us (21%)
  blocking collectives  64.5 us (5%)
  local copies, waits for them, and re-layouts  60.7 us (4%)
  other arithmetic  32.5 us (2%)
  starting transfers between devices  18 us (1%)
  between operations  15.1 us (1%)
    reduce_scatter x7, waiting for transfers between devices, reduce_grads(): partial_sum = lax.psum_scatter(grads, 'dp', scatter_dimension=0, tiled=True)  795 us
    reduce_scatter x7, waiting for transfers between devices, reduce_grads(): return lax.psum_scatter(partial_sum, 'seq', scatter_dimension=1, tiled=True)  69.4 us
    dot_general x2, matrix products, attend_back(): jnp.einsum('hgqk,khd->qhgd', d_scores, key_all, preferred_element_type=f32)  51 us
    dot_general x2, matrix products, attend_back(): jnp.einsum('hgqk,qhgd->khd', d_scores, query_block, preferred_element_typ...  46 us
    psum x1, blocking collectives, body(): lax.psum((jnp.sum(attn_gain_terms, axis=0), jnp.sum(query_gain_terms, axi...  32.5 us
  transfers between devices with their start and end apart: 18, of which 13 were waited for; matrix products, arithmetic and copies ran while one was open for 6% of the time, Pallas kernels for 0%

profile of v1, /device:TPU:0, one launch (start us, length us, event | category | flops | bytes accessed | tf_op | source)
XLA Modules:
  0.0 1397.9 jit_solution(13141782732980944463)
XLA Ops:
  11.9 3.1 multiply_reduce_fusion.8
  19.7 4.4 all-to-all-start.1
  24.1 3.9 copy.93
  28.1 3.0 multiply_reduce_fusion.5
  33.8 5.5 all-to-all-done.1
  39.2 4.6 all-to-all-start
  44.2 2.3 copy.124
  49.3 7.9 all-to-all-done
  57.3 3.3 copy.125
  60.5 2.6 reshape.334
  64.2 36.4 %while.28 = (s32[]{:T(128)}, bf16[2,512,4,2,64]{1,4,3,2,0:T(8,128)(2,1)}, f32[2,4,2,512]{3,2,1,0:T(2,128)S(1)}, s32[2]{0:T(128)S(1)}, s32[1024]{0:T(1024)S(1)}, ...) while((s32[]{:T(128)}, ...), condition=%wide.region_8.9_spmd.clone, body=%wide.region_5.8_spmd.clone.sunk | while | flops 1125904896 | bytes 54672044 | solution.py:127
  68.0 4.4 bitcast_reduce_fusion.2
  72.5 4.3 fusion.161
  76.8 5.6 fusion.162
  86.3 4.4 bitcast_reduce_fusion.2
  90.7 4.3 fusion.161
  95.0 5.6 fusion.162
  100.6 6.1 copy.115
  106.7 5.1 reshape.352
  111.8 4.8 all-to-all-start.2
  116.7 12.4 all-to-all-done.2
  129.1 2.3 copy.99
  133.8 2.7 multiply_reduce_fusion.4
  138.3 7.5 fusion.102
  145.8 7.5 fusion.103
  153.3 20.4 %multiply_convert_fusion = (bf16[512,4608]{1,0:T(8,128)(2,1)}, bf16[512,4608]{1,0:T(8,128)(2,1)}, bf16[512,4608]{1,0:T(8,128)(2,1)}) fusion(f32[512,4608]{1,0:T(8,128)} %fusion.102, f32[512,4608]{1,0:T(8,128)} %fusion.103, bf16[4608,1024]{1,0:T(8,128)(2,1)} %param.31, bf16[1,512,1024]{2,1,0:T(8,128)(2,1)S(1)} %copy-done.27), kind=kOutput, calls=%fused_computation.63 | convolution fusion | flops 4869586944 | bytes 43515904 | tf_op jit(solution)/shard_map/td,fd->tf/dot_general | solution.py:140
  173.7 9.2 fusion.104
  182.9 8.8 multiply_reduce_fusion
  194.9 3.6 all-to-all-start.3
  198.5 11.4 all-to-all-done.3
  214.9 155.5 %while.29 = (s32[]{:T(128)}, f32[1024,4,64]{0,2,1:T(8,128)}, f32[1024,4,64]{0,2,1:T(8,128)S(1)}, bf16[2,512,4,2,64]{1,4,3,2,0:T(8,128)(2,1)}, s32[2]{0:T(128)S(1...) while((s32[]{:T(128)}, f32[1024,4,64]{0,2,1:T(8,128)}, ...), condition=%wide.region_13.14_spmd.clone, body=%wide.region_11.13_spmd.clone.sunk | while | flops 2745969152 | bytes 194050784 | solution.py:186
  218.8 9.6 fusion.172
  228.3 8.2 fusion.173
  236.5 25.5 %fusion.176 = bf16[2,512,4,2,64]{1,4,3,2,0:T(8,128)(2,1)} fusion(bf16[2,512,4,2,64]{1,4,3,2,0:T(8,128)(2,1)} %get-tuple-element.438, s32[]{:T(128)} %get-tuple-element.435, f32[4,2,512,1024]{3,2,1,0:T(8,128)} %fusion.172, f32[4,512,2,1024]{3,1,2,0:T(8,128)} %fusion.173, bf16[1024,4,64]{0,2,1:T(8,128)(2,1)S(1)} %get-tuple-element.456), kind=kOutput, calls=%fused_computation.44.clone.1 | convolution fusion | flops 558109696 | bytes 68157952 | tf_op jit(solution)/shard_map/while/body/eval_jaxpr/hgqk,khd->qhgd/dot_general | solution.py:176
  262.1 22.8 %fusion.174 = f32[1024,4,64]{0,2,1:T(8,128)} fusion(f32[4,2,512,1024]{3,2,1,0:T(8,128)} %fusion.172, f32[4,512,2,1024]{3,1,2,0:T(8,128)} %fusion.173, f32[1024,4,64]{0,2,1:T(8,128)} %get-tuple-element.436, pred[]{:T(512)S(6)} %compare.3, bf16[1024,4,2,64]{0,3,2,1:T(8,128)(2,1)} %get-tuple-element.454, s32[]{:T(128)S(6)} %select_n.56), kind=kOutput, calls=%fused_computation.39.clone.1 | convolution fusion | flops 558371840 | bytes 69730312 | tf_op jit(solution)/shard_map/while/body/eval_jaxpr/hgqk,qhgd->khd/dot_general | solution.py:177
  284.9 7.6 fusion.175
  296.3 9.6 fusion.172
  305.9 8.2 fusion.173
  314.1 25.5 %fusion.176 = bf16[2,512,4,2,64]{1,4,3,2,0:T(8,128)(2,1)} fusion(bf16[2,512,4,2,64]{1,4,3,2,0:T(8,128)(2,1)} %get-tuple-element.438, s32[]{:T(128)} %get-tuple-element.435, f32[4,2,512,1024]{3,2,1,0:T(8,128)} %fusion.172, f32[4,512,2,1024]{3,1,2,0:T(8,128)} %fusion.173, bf16[1024,4,64]{0,2,1:T(8,128)(2,1)S(1)} %get-tuple-element.456), kind=kOutput, calls=%fused_computation.44.clone.1 | convolution fusion | flops 558109696 | bytes 68157952 | tf_op jit(solution)/shard_map/while/body/eval_jaxpr/hgqk,khd->qhgd/dot_general | solution.py:176
  339.6 23.2 %fusion.174 = f32[1024,4,64]{0,2,1:T(8,128)} fusion(f32[4,2,512,1024]{3,2,1,0:T(8,128)} %fusion.172, f32[4,512,2,1024]{3,1,2,0:T(8,128)} %fusion.173, f32[1024,4,64]{0,2,1:T(8,128)} %get-tuple-element.436, pred[]{:T(512)S(6)} %compare.3, bf16[1024,4,2,64]{0,3,2,1:T(8,128)(2,1)} %get-tuple-element.454, s32[]{:T(128)S(6)} %select_n.56), kind=kOutput, calls=%fused_computation.39.clone.1 | convolution fusion | flops 558371840 | bytes 69730312 | tf_op jit(solution)/shard_map/while/body/eval_jaxpr/hgqk,qhgd->khd/dot_general | solution.py:177
  362.8 7.6 fusion.175
  372.6 13.2 all_to_all.90
  391.5 3.5 fusion.85
  395.1 4.5 fusion.91
  399.7 4.6 copy.116
  406.1 13.2 all_to_all.91
  426.2 3.4 fusion.83
  430.9 11.6 fusion.107
  442.5 11.8 fusion.108
  455.6 11.7 fusion.75
  468.1 49.3 %reduce-scatter.23.cloned.1.call-done = f32[64,512]{1,0:T(8,128)} async-done(((f32[1024,512]{1,0:T(8,128)}), f32[64,512]{1,0:T(8,128)}) %reduce-scatter.23.cloned.1.call-update) | async-done | bytes 131088 | tf_op jit(solution)/shard_map/reduce_scatter | solution.py:41
  517.5 75.5 %reduce-scatter.27.cloned.1.call-done = f32[64,1024]{1,0:T(8,128)} async-done(((f32[1024,1024]{1,0:T(8,128)}), f32[64,1024]{1,0:T(8,128)}) %reduce-scatter.27.cloned.1.call-update) | async-done | bytes 262160 | tf_op jit(solution)/shard_map/reduce_scatter | solution.py:41
  593.0 76.1 %reduce-scatter.15.cloned.1.call-done = f32[64,1024]{1,0:T(8,128)} async-done(((f32[1024,1024]{1,0:T(8,128)}), f32[64,1024]{1,0:T(8,128)}) %reduce-scatter.15.cloned.1.call-update) | async-done | bytes 262160 | tf_op jit(solution)/shard_map/reduce_scatter | solution.py:41
  669.1 197.8 %reduce-scatter.31.cloned.1.call-done = f32[64,4608]{1,0:T(8,128)} async-done(((f32[1024,4608]{1,0:T(8,128)}), f32[64,4608]{1,0:T(8,128)}) %reduce-scatter.31.cloned.1.call-update) | async-done | bytes 1179664 | tf_op jit(solution)/shard_map/reduce_scatter | solution.py:41
  867.1 197.9 %reduce-scatter.35.cloned.1.call-done = f32[64,4608]{1,0:T(8,128)} async-done(((f32[1024,4608]{1,0:T(8,128)}), f32[64,4608]{1,0:T(8,128)}) %reduce-scatter.35.cloned.1.call-update) | async-done | bytes 1179664 | tf_op jit(solution)/shard_map/reduce_scatter | solution.py:41
  1065.1 198.1 %reduce-scatter.39.cloned.1.call-done = f32[288,1024]{1,0:T(8,128)} async-done(((f32[4608,1024]{1,0:T(8,128)}), f32[288,1024]{1,0:T(8,128)}) %reduce-scatter.39.cloned.1.call-update) | async-done | bytes 1179664 | tf_op jit(solution)/shard_map/reduce_scatter | solution.py:41
  1263.2 10.1 add_bitcast_fusion
  1276.5 2.6 fusion.69
  1279.1 32.5 %all-reduce = (f32[1024]{0:T(1024)S(1)}, f32[64]{0:T(128)S(1)}, f32[64]{0:T(128)S(1)}, f32[1024]{0:T(1024)S(1)}) all-reduce(f32[1024]{0:T(1024)S(1)} %get-tuple-element.190, f32[64]{0:T(128)S(1)} %get-tuple-element.186, f32[64]{0:T(128)S(1)} %get-tuple-element.192, f32[1024]{0:T(1024)S(1)} %copy-done.46), channel_id=1, replica_groups=mesh['dp'=16,'seq'=2] {'dp'}, use_global_device_ids=true, to_apply=%region_18.19 | all-reduce | flops 2176 | bytes 17408 | tf_op jit(solution)/shard_map/psum | solution.py:212
  1311.6 5.7 all-reduce.1
  1317.3 4.2 fusion.68
  1321.5 20.3 %reduce-scatter.33.cloned.1.call-done = f32[64,2304]{1,0:T(8,128)} async-done(((f32[64,4608]{1,0:T(8,128)}), f32[64,2304]{1,0:T(8,128)}) %reduce-scatter.33.cloned.1.call-update) | async-done | bytes 589840 | tf_op jit(solution)/shard_map/reduce_scatter | solution.py:42
  1341.8 24.7 %reduce-scatter.37.cloned.1.call-done = f32[64,2304]{1,0:T(8,128)} async-done(((f32[64,4608]{1,0:T(8,128)}), f32[64,2304]{1,0:T(8,128)}) %reduce-scatter.37.cloned.1.call-update) | async-done | bytes 589840 | tf_op jit(solution)/shard_map/reduce_scatter | solution.py:42
  1366.5 24.4 %reduce-scatter.41.cloned.1.call-done = f32[288,512]{1,0:T(8,128)} async-done(((f32[288,1024]{1,0:T(8,128)}), f32[288,512]{1,0:T(8,128)}) %reduce-scatter.41.cloned.1.call-update) | async-done | bytes 589840 | tf_op jit(solution)/shard_map/reduce_scatter | solution.py:42
  (224 shorter events, 59.5 us)
Async XLA Ops:
  7.2 126.6 %copy-start = (bf16[1024,1024]{1,0:T(8,128)(2,1)S(1)}, bf16[1024,1024]{1,0:T(8,128)(2,1)}, u32[]{:S(2)}) copy-start(bf16[1024,1024]{1,0:T(8,128)(2,1)} %param.27) | copy-start | bytes 6291460
  7.2 4.7 copy-start.2
  8.9 19.2 %copy-start.40 = (f32[512]{0:T(512)}, f32[512]{0:T(512)S(1)}, u32[]{:S(2)}) copy-start(f32[512]{0:T(512)S(1)} %add_rsqrt_fusion.3) | copy-start | bytes 6148
  9.6 18.5 %copy-start.38 = (f32[1024]{0:T(1024)}, f32[1024]{0:T(1024)S(1)}, u32[]{:S(2)}) copy-start(f32[1024]{0:T(1024)S(1)} %convert_element_type.137) | copy-start | bytes 12292
  11.9 3.1 copy-start.49
  15.0 3.4 copy-start.36
  15.0 3.4 copy-start.44
  15.0 3.1 copy-start.16
  18.1 13.5 copy-start.24
  19.7 19.6 %all-to-all-start.1 = ((bf16[512,8,128]{0,2,1:T(8,128)(2,1)}), bf16[512,8,128]{0,2,1:T(8,128)(2,1)}, u32[]{:S(2)}, u32[]{:S(2)}) async-start(bf16[512,8,128]{0,2,1:T(8,128)(2,1)} %pad_maximum_fusion.2), calls=%async_computation.1 | async-start | bytes 2097152 | tf_op jit(solution)/shard_map/all_to_all | solution.py:96
  28.1 3.0 copy-start.50
  31.0 1.3 copy-start.7
  32.7 11.2 copy-start.51
  39.2 18.0 %all-to-all-start = ((bf16[512,8,128]{0,2,1:T(8,128)(2,1)}), bf16[512,8,128]{0,2,1:T(8,128)(2,1)}, u32[]{:S(2)}, u32[]{:S(2)}) async-start(bf16[512,8,128]{0,2,1:T(8,128)(2,1)} %bitcast.7), calls=%async_computation | async-start | bytes 2097152 | tf_op jit(solution)/shard_map/all_to_all | solution.py:95
  100.6 11.2 copy-start.5
  100.6 11.2 copy-start.34
  106.7 10.0 copy-start.47
  111.8 17.3 %all-to-all-start.2 = ((bf16[1024,4,128]{2,1,0:T(4,128)(2,1)}), bf16[1024,4,128]{2,1,0:T(4,128)(2,1)}, u32[]{:S(2)}, u32[]{:S(2)}) async-start(bf16[1024,4,128]{2,1,0:T(4,128)(2,1)} %reshape.352), calls=%async_computation.2 | async-start | bytes 2097152 | tf_op jit(solution)/shard_map/all_to_all | solution.py:129
  116.7 17.1 %copy-start.3 = (bf16[1,512,1024]{2,1,0:T(8,128)(2,1)S(1)}, bf16[1,512,1024]{2,1,0:T(8,128)(2,1)}, u32[]{:S(2)}) copy-start(bf16[1,512,1024]{2,1,0:T(8,128)(2,1)} %param.18) | copy-start | bytes 3145732
  133.8 4.6 copy-start.48
  136.5 1.3 copy-start.11
  137.8 8.0 slice-start
  138.3 7.5 copy-start.14
  138.3 7.5 slice-start.1
  138.3 7.5 slice-start.2
  145.8 7.5 copy-start.27
  173.7 9.2 copy-start.12
  173.7 9.2 copy-start.21
  192.3 1.4 copy-start.9
  194.9 15.0 %all-to-all-start.3 = ((bf16[512,8,128]{2,0,1:T(8,128)(2,1)}), bf16[512,8,128]{2,0,1:T(8,128)(2,1)S(1)}, u32[]{:S(2)}, u32[]{:S(2)}) async-start(bf16[512,8,128]{2,0,1:T(8,128)(2,1)} %bitcast.254), calls=%async_computation.3 | async-start | bytes 2097152 | tf_op jit(solution)/shard_map/all_to_all | solution.py:159
  198.4 268.9 %reduce-scatter.19.cloned.1.call-start = ((), (), s32[]{:S(2)}) async-start(), calls=%async_computation.22 | async-start | bytes 2228224 | tf_op jit(solution)/shard_map/reduce_scatter | solution.py:41
  211.9 3.0 copy-start.6
  211.9 3.0 copy-start.35
  385.8 1.7 copy-start.25
  385.8 1.7 copy-start.31
  386.5 1.4 copy-start.17
  386.5 1.4 copy-start.37
  386.5 1.4 copy-start.45
  388.7 2.8 copy-start.19
  391.5 125.9 %reduce-scatter.23.cloned.1.call-start = ((), (), s32[]{:S(2)}) async-start(), calls=%async_computation.24 | async-start | bytes 2228224 | tf_op jit(solution)/shard_map/reduce_scatter | solution.py:41
  391.5 3.6 copy-start.10
  395.1 197.9 %reduce-scatter.27.cloned.1.call-start = ((), (), s32[]{:S(2)}) async-start(), calls=%async_computation.26 | async-start | bytes 4456448 | tf_op jit(solution)/shard_map/reduce_scatter | solution.py:41
  399.7 269.4 %reduce-scatter.15.cloned.1.call-start = ((), (), s32[]{:S(2)}) async-start(), calls=%async_computation.20 | async-start | bytes 4456448 | tf_op jit(solution)/shard_map/reduce_scatter | solution.py:41
  421.4 2.2 copy-start.8
  421.4 2.2 copy-start.33
  421.4 2.2 copy-start.43
  429.7 437.3 %reduce-scatter.31.cloned.1.call-start = ((), (), s32[]{:S(2)}) async-start(), calls=%async_computation.28 | async-start | bytes 20054016 | tf_op jit(solution)/shard_map/reduce_scatter | solution.py:41
  442.5 622.5 %reduce-scatter.35.cloned.1.call-start = ((), (), s32[]{:S(2)}) async-start(), calls=%async_computation.30 | async-start | bytes 20054016 | tf_op jit(solution)/shard_map/reduce_scatter | solution.py:41
  454.4 808.8 %reduce-scatter.39.cloned.1.call-start = ((), (), s32[]{:S(2)}) async-start(), calls=%async_computation.32 | async-start | bytes 20054016 | tf_op jit(solution)/shard_map/reduce_scatter | solution.py:41
  467.3 854.2 %reduce-scatter.21.cloned.1.call-start = ((), (), s32[]{:S(2)}) async-start(), calls=%async_computation.23 | async-start | bytes 196608 | tf_op jit(solution)/shard_map/reduce_scatter | solution.py:42
  468.0 853.5 %reduce-scatter.25.cloned.1.call-start = ((), (), s32[]{:S(2)}) async-start(), calls=%async_computation.25 | async-start | bytes 196608 | tf_op jit(solution)/shard_map/reduce_scatter | solution.py:42
  517.4 745.8 %copy-start.13 = (f32[512,1024]{1,0:T(8,128)S(1)}, f32[512,1024]{1,0:T(8,128)}, u32[]{:S(2)}) copy-start(f32[512,1024]{1,0:T(8,128)} %copy-done.11) | copy-start | bytes 6291460
  517.4 804.1 %reduce-scatter.29.cloned.1.call-start = ((), (), s32[]{:S(2)}) async-start(), calls=%async_computation.27 | async-start | bytes 393216 | tf_op jit(solution)/shard_map/reduce_scatter | solution.py:42
  592.9 728.6 %reduce-scatter.17.cloned.1.call-start = ((), (), s32[]{:S(2)}) async-start(), calls=%async_computation.21 | async-start | bytes 393216 | tf_op jit(solution)/shard_map/reduce_scatter | solution.py:42
  669.1 672.7 %reduce-scatter.33.cloned.1.call-start = ((), (), s32[]{:S(2)}) async-start(), calls=%async_computation.29 | async-start | bytes 1769472 | tf_op jit(solution)/shard_map/reduce_scatter | solution.py:42
  867.0 499.5 %reduce-scatter.37.cloned.1.call-start = ((), (), s32[]{:S(2)}) async-start(), calls=%async_computation.31 | async-start | bytes 1769472 | tf_op jit(solution)/shard_map/reduce_scatter | solution.py:42
  1065.0 325.9 %reduce-scatter.41.cloned.1.call-start = ((), (), s32[]{:S(2)}) async-start(), calls=%async_computation.33 | async-start | bytes 1769472 | tf_op jit(solution)/shard_map/reduce_scatter | solution.py:42
  1263.2 10.1 copy-start.20
  1263.2 10.1 copy-start.22
  1273.2 1.6 copy-start.23
  1273.3 1.9 copy-start.30
  1275.1 1.4 copy-start.26
  1276.5 2.6 copy-start.46
  1317.3 73.7 %copy-start.1 = (bf16[1024,1024]{1,0:T(8,128)(2,1)S(1)}, bf16[1024,1024]{1,0:T(8,128)(2,1)}, u32[]{:S(2)}) copy-start(bf16[1024,1024]{1,0:T(8,128)(2,1)} %param.27) | copy-start | bytes 6291460
  (9 other events, 11.0 us)
Sparse Core Ops, SparseCore 0:
  391.6 60.9 reduce-scatter.18
  456.8 60.5 reduce-scatter.22
  521.3 71.6 reduce-scatter.26
  597.1 71.9 reduce-scatter.14
  673.0 193.9 reduce-scatter.30
  871.0 193.9 reduce-scatter.34
  1069.1 193.9 reduce-scatter.38
  1265.9 9.3 reduce-scatter.20
  1278.1 10.2 reduce-scatter.24
  1291.0 11.6 reduce-scatter.28
  1305.6 11.6 reduce-scatter.16
  1320.0 21.7 reduce-scatter.32
  1344.7 21.7 reduce-scatter.36
  1369.2 21.7 reduce-scatter.40
